TPU v7x, 32 devices: a whole 2x2x4 slice. The times are simulated.
32 devices in a mesh: seq: 8 (over z, core), head: 4 (over y, x).
Axes of the slice: x: 2, y: 2, z: 4, core: 2. Of those that a mesh axis runs over, the one named last changes fastest.
Arguments:
- video_query: bfloat16 [4096, 3072], P(('seq', 'head')), may hold values from -8 to 8
- video_key: bfloat16 [4096, 3072], P(('seq', 'head')), may hold values from -8 to 8
- video_value: bfloat16 [4096, 3072], P(('seq', 'head')), may hold values from -6 to 6
- video_grad: bfloat16 [4096, 3072], P(('seq', 'head')), may hold values from -6 to 6
- text_query: bfloat16 [256, 3072], P(None, 'head'), may hold values from -8 to 8
- text_key: bfloat16 [256, 3072], P(None, 'head'), may hold values from -8 to 8
- text_value: bfloat16 [256, 3072], P(None, 'head'), may hold values from -6 to 6
- text_grad: bfloat16 [256, 3072], P(None, 'head'), may hold values from -6 to 6
- tile_list: int32 [32, 8], replicated, may hold values from 0 to 31, as said below
- tile_count: int32 [32], replicated, may hold values from 1 to 8, as said below
- text_mask: int32 [256], replicated, may hold values from 0 to 1, as said below
Outputs:
- attended_video: bfloat16 [4096, 3072], P(('seq', 'head'))
- video_query_grad: bfloat16 [4096, 3072], P(('seq', 'head'))
- video_key_grad: bfloat16 [4096, 3072], P(('seq', 'head'))
- video_value_grad: bfloat16 [4096, 3072], P(('seq', 'head'))
- attended_text: bfloat16 [256, 3072], P(None, 'head')
- text_query_grad: bfloat16 [256, 3072], P(None, 'head')
- text_key_grad: bfloat16 [256, 3072], P(None, 'head')
- text_value_grad: bfloat16 [256, 3072], P(None, 'head')
Inputs may be any that keep to these rules, and one draw needn't show every extreme that they name: `tile_list`: the 8 entries of one query tile's list are distinct. Query tiles fall in aligned blocks of 4; the used entries of one block together name at most 2 distinct tiles of any other block of 4 tiles, and every block names exactly 2 from some other block. `tile_count`: every aligned block of 4 query tiles has a tile that uses all 8 entries. `text_mask`: the ones form a prefix of at least 64 entries.
All inputs are finite; a program needn't handle non-finite values.
Results may differ from a plain program's by a relative error of at most 0.012.
Values may be sent and summed in bfloat16 or wider, within the bound.
A program may use at most 192 MiB of HBM per device.

v0:
```python
import jax
import jax.numpy as jnp
from jax import lax
from jax.sharding import PartitionSpec as P

HD = 128
TXT = 256
TILE = 128
KT = 8
MOST = 2
NEGATIVE = -1e30
HIGHEST_PRECISION = lax.Precision.HIGHEST


def split_product(form, weights, data):
    upper = weights.astype(jnp.bfloat16)
    lower = (weights - upper.astype(jnp.float32)).astype(jnp.bfloat16)
    return jnp.einsum(form, upper, data, preferred_element_type=jnp.float32) + jnp.einsum(
        form, lower, data, preferred_element_type=jnp.float32
    )


def block_scores(query_blk, key_blk, live_blk, factor):
    scores = (
        jnp.einsum("bthd,bkhd->bhtk", query_blk, key_blk, preferred_element_type=jnp.float32)
        * factor
    )
    scores = jnp.where(live_blk[:, None, None, :], scores, NEGATIVE)
    maximum = jnp.max(scores, axis=-1)
    log_total = maximum + jnp.log(jnp.sum(jnp.exp(scores - maximum[..., None]), axis=-1))
    return (scores, log_total)


def block_forward(scores, log_total, value_blk, grad_blk):
    weights = jnp.exp(scores - log_total[..., None]).astype(jnp.bfloat16)
    output = jnp.einsum("bhtk,bkhd->bthd", weights, value_blk, preferred_element_type=jnp.float32)
    offset = jnp.sum(grad_blk.astype(jnp.float32) * output, axis=-1)
    return (output, jnp.transpose(offset, (0, 2, 1)))


def block_backward(scores, log_total, offset, query_blk, key_blk, value_blk, grad_blk, factor):
    probability = jnp.exp(scores - log_total[..., None])
    weights = probability.astype(jnp.bfloat16)
    prob_grad = jnp.einsum(
        "bthd,bkhd->bhtk", grad_blk, value_blk, preferred_element_type=jnp.float32
    )
    score_grad = (probability * (prob_grad - offset[..., None])).astype(jnp.bfloat16)
    query_grad = (
        jnp.einsum("bhtk,bkhd->bthd", score_grad, key_blk, preferred_element_type=jnp.float32)
        * factor
    )
    key_grad = (
        jnp.einsum("bhtk,bthd->bkhd", score_grad, query_blk, preferred_element_type=jnp.float32)
        * factor
    )
    value_grad = jnp.einsum(
        "bhtk,bthd->bkhd", weights, grad_blk, preferred_element_type=jnp.float32
    )
    return (query_grad, key_grad, value_grad)


def spread_grads(pool_total, text_total, grad_blk, pool_slot):
    block_tiles = grad_blk.shape[0]
    tile_part = grad_blk[:, : KT * TILE].reshape(block_tiles, KT, TILE, pool_total.shape[2])
    return (
        pool_total.at[pool_slot].add(tile_part),
        text_total + jnp.sum(grad_blk[:, KT * TILE :], axis=0),
    )


def body(
    video_query,
    video_key,
    video_value,
    video_grad,
    text_query,
    text_key,
    text_value,
    text_grad,
    tile_list,
    tile_count,
    text_mask,
):
    factor = HD ** (-0.5)
    groups = lax.axis_size("seq")
    own_group = lax.axis_index("seq")
    query_rows, key_rows, value_rows, grad_rows = (
        lax.all_to_all(video_query, "head", split_axis=1, concat_axis=0, tiled=True),
        lax.all_to_all(video_key, "head", split_axis=1, concat_axis=0, tiled=True),
        lax.all_to_all(video_value, "head", split_axis=1, concat_axis=0, tiled=True),
        lax.all_to_all(video_grad, "head", split_axis=1, concat_axis=0, tiled=True),
    )
    token_rows, feature_width = query_rows.shape
    head_count = feature_width // HD
    shard_tiles = token_rows // TILE
    tile_total = tile_list.shape[0]
    text_ok = text_mask > 0
    entry_live = jnp.arange(KT)[None, :] < tile_count[:, None]
    tile_hits = (tile_list[:, :, None] == jnp.arange(tile_total)[None, None, :]) & entry_live[
        :, :, None
    ]
    wanted = jnp.any(
        jnp.any(tile_hits, axis=1).reshape(groups, shard_tiles, tile_total), axis=1
    ).reshape(groups, groups, shard_tiles)
    slot_rank = jnp.cumsum(wanted.astype(jnp.int32), axis=2) - 1
    distinct = (jnp.arange(groups)[:, None] != jnp.arange(groups)[None, :])[:, :, None, None]
    select = (
        wanted[:, :, None, :]
        & (slot_rank[:, :, None, :] == jnp.arange(MOST)[None, None, :, None])
        & distinct
    )
    outgoing = lax.dynamic_index_in_dim(select, own_group, 1, keepdims=False)
    incoming = lax.dynamic_index_in_dim(select, own_group, 0, keepdims=False)
    picker = outgoing.reshape(groups * MOST, shard_tiles).astype(jnp.bfloat16)
    send_keys = jnp.dot(
        picker,
        key_rows.reshape(shard_tiles, TILE * feature_width),
        preferred_element_type=jnp.float32,
    )
    send_keys = send_keys.astype(jnp.bfloat16).reshape(groups, MOST * TILE, feature_width)
    send_values = jnp.dot(
        picker,
        value_rows.reshape(shard_tiles, TILE * feature_width),
        preferred_element_type=jnp.float32,
    )
    send_values = send_values.astype(jnp.bfloat16).reshape(groups, MOST * TILE, feature_width)
    owner_base = (
        jnp.arange(groups, dtype=jnp.int32)[:, None, None] * shard_tiles
        + jnp.arange(shard_tiles, dtype=jnp.int32)[None, None, :]
    )
    slot_ids = jnp.where(
        jnp.any(incoming, axis=2), jnp.sum(jnp.where(incoming, owner_base, 0), axis=2), -1
    ).reshape(groups * MOST)
    pool_ids = jnp.concatenate(
        [own_group * shard_tiles + jnp.arange(shard_tiles, dtype=jnp.int32), slot_ids]
    )
    pool_size = shard_tiles + groups * MOST
    my_list = lax.dynamic_slice_in_dim(tile_list, own_group * shard_tiles, shard_tiles, 0)
    my_count = lax.dynamic_slice_in_dim(tile_count, own_group * shard_tiles, shard_tiles, 0)
    pool_match = my_list[:, :, None] == pool_ids[None, None, :]
    pool_slot = jnp.sum(jnp.where(pool_match, jnp.arange(pool_size, dtype=jnp.int32), 0), axis=2)
    live_entry = jnp.any(pool_match, axis=2) & (jnp.arange(KT)[None, :] < my_count[:, None])
    text_query3 = text_query.reshape(TXT, head_count, HD)
    text_key3 = text_key.reshape(TXT, head_count, HD)
    text_value3 = text_value.reshape(TXT, head_count, HD)
    text_grad3 = text_grad.reshape(TXT, head_count, HD)
    block_tiles = min(shard_tiles, max(1, 512 // TILE))
    block_count = shard_tiles // block_tiles
    query_blocks = query_rows.reshape(block_count, block_tiles, TILE, head_count, HD)
    grad_blocks = grad_rows.reshape(block_count, block_tiles, TILE, head_count, HD)
    slot_blocks = pool_slot.reshape(block_count, block_tiles, KT)
    live_blocks = jnp.concatenate(
        [
            jnp.repeat(live_entry, TILE, axis=1),
            jnp.broadcast_to(text_ok[None, :], (shard_tiles, TXT)),
        ],
        axis=1,
    )
    live_blocks = live_blocks.reshape(block_count, block_tiles, KT * TILE + TXT)
    local_keys = key_rows.reshape(shard_tiles, TILE, feature_width)
    local_values = value_rows.reshape(shard_tiles, TILE, feature_width)

    def build_pool(received):
        got_keys, got_values = received
        return (
            jnp.concatenate(
                [local_keys, got_keys.reshape(groups * MOST, TILE, feature_width)], axis=0
            ),
            jnp.concatenate(
                [local_values, got_values.reshape(groups * MOST, TILE, feature_width)], axis=0
            ),
        )

    def block_rows(pool, slot_blk, text_part):
        picked = pool[slot_blk].reshape(block_tiles, KT * TILE, head_count, HD)
        return jnp.concatenate(
            [picked, jnp.broadcast_to(text_part[None], (block_tiles, TXT, head_count, HD))], axis=1
        )

    pool_keys, pool_values = build_pool(
        (
            lax.all_to_all(send_keys, "seq", split_axis=0, concat_axis=0, tiled=True),
            lax.all_to_all(send_values, "seq", split_axis=0, concat_axis=0, tiled=True),
        )
    )
    start = (
        jnp.zeros((pool_size, TILE, feature_width), jnp.float32),
        jnp.zeros((pool_size, TILE, feature_width), jnp.float32),
        jnp.zeros((TXT, head_count, HD), jnp.float32),
        jnp.zeros((TXT, head_count, HD), jnp.float32),
    )

    def forward_step(running, inputs):
        query_blk, grad_blk, slot_blk, live_blk = inputs
        key_blk = block_rows(pool_keys, slot_blk, text_key3)
        value_blk = block_rows(pool_values, slot_blk, text_value3)
        scores, log_total = block_scores(query_blk, key_blk, live_blk, factor)
        output, offset = block_forward(scores, log_total, value_blk, grad_blk)
        return (running, (output.astype(jnp.bfloat16), log_total, offset))

    unused, forwards = lax.scan(
        forward_step, None, (query_blocks, grad_blocks, slot_blocks, live_blocks)
    )
    attended_blocks, total_blocks, offset_blocks = forwards
    again_keys, again_values = build_pool(
        (
            lax.all_to_all(send_keys, "seq", split_axis=0, concat_axis=0, tiled=True),
            lax.all_to_all(send_values, "seq", split_axis=0, concat_axis=0, tiled=True),
        )
    )

    def backward_step(running, inputs):
        key_acc, value_acc, text_key_acc, text_value_acc = running
        query_blk, grad_blk, slot_blk, live_blk, log_total, offset = inputs
        key_blk = block_rows(again_keys, slot_blk, text_key3)
        value_blk = block_rows(again_values, slot_blk, text_value3)
        scores, unused_total = block_scores(query_blk, key_blk, live_blk, factor)
        query_grad, key_grad, value_grad = block_backward(
            scores, log_total, offset, query_blk, key_blk, value_blk, grad_blk, factor
        )
        key_acc, text_key_acc = spread_grads(key_acc, text_key_acc, key_grad, slot_blk)
        value_acc, text_value_acc = spread_grads(value_acc, text_value_acc, value_grad, slot_blk)
        return ((key_acc, value_acc, text_key_acc, text_value_acc), query_grad.astype(jnp.bfloat16))

    finals, query_grad_blocks = lax.scan(
        backward_step,
        start,
        (query_blocks, grad_blocks, slot_blocks, live_blocks, total_blocks, offset_blocks),
    )
    key_acc, value_acc, text_key_acc, text_value_acc = finals
    back_keys, back_values = (
        lax.all_to_all(
            key_acc[shard_tiles:].reshape(groups, MOST * TILE, feature_width),
            "seq",
            split_axis=0,
            concat_axis=0,
            tiled=True,
        ),
        lax.all_to_all(
            value_acc[shard_tiles:].reshape(groups, MOST * TILE, feature_width),
            "seq",
            split_axis=0,
            concat_axis=0,
            tiled=True,
        ),
    )
    out_flat = outgoing.reshape(groups * MOST, shard_tiles)
    target_tile = jnp.where(
        jnp.any(out_flat, axis=1),
        jnp.sum(jnp.where(out_flat, jnp.arange(shard_tiles, dtype=jnp.int32)[None, :], 0), axis=1),
        shard_tiles,
    )
    own_key_grad = (
        key_acc[:shard_tiles]
        .at[target_tile]
        .add(back_keys.reshape(groups * MOST, TILE, feature_width), mode="drop")
    )
    own_value_grad = (
        value_acc[:shard_tiles]
        .at[target_tile]
        .add(back_values.reshape(groups * MOST, TILE, feature_width), mode="drop")
    )
    key_rows3 = key_rows.reshape(token_rows, head_count, HD)
    value_rows3 = value_rows.reshape(token_rows, head_count, HD)
    text_query32 = text_query3.astype(jnp.float32)
    text_key32 = text_key3.astype(jnp.float32)
    text_value32 = text_value3.astype(jnp.float32)
    text_grad32 = text_grad3.astype(jnp.float32)
    video_scores = (
        jnp.einsum("thd,khd->htk", text_query3, key_rows3, preferred_element_type=jnp.float32)
        * factor
    )
    text_scores = (
        jnp.einsum("thd,khd->htk", text_query3, text_key3, preferred_element_type=jnp.float32)
        * factor
    )
    text_scores = jnp.where(text_ok[None, None, :], text_scores, NEGATIVE)
    maximum = jnp.maximum(
        lax.pmax(jnp.max(video_scores, axis=-1), "seq"), jnp.max(text_scores, axis=-1)
    )
    video_exp = jnp.exp(video_scores - maximum[..., None])
    denominator, numerator = lax.psum(
        (jnp.sum(video_exp, axis=-1), split_product("htk,khd->thd", video_exp, value_rows3)), "seq"
    )
    text_exp = jnp.exp(text_scores - maximum[..., None])
    denominator = denominator + jnp.sum(text_exp, axis=-1)
    numerator = numerator + jnp.einsum(
        "htk,khd->thd", text_exp, text_value32, precision=HIGHEST_PRECISION
    )
    log_total = maximum + jnp.log(denominator)
    text_out = numerator / denominator.T[:, :, None]
    video_prob = jnp.exp(video_scores - log_total[..., None])
    text_prob = jnp.exp(text_scores - log_total[..., None])
    text_offset = jnp.sum(text_grad32 * text_out, axis=-1).T
    video_dscore = video_prob * (
        jnp.einsum("thd,khd->htk", text_grad3, value_rows3, preferred_element_type=jnp.float32)
        - text_offset[..., None]
    )
    text_dscore = text_prob * (
        jnp.einsum("thd,khd->htk", text_grad3, text_value3, preferred_element_type=jnp.float32)
        - text_offset[..., None]
    )
    query_part = split_product("htk,khd->thd", video_dscore, key_rows3) * factor
    video_key_from_text = split_product("htk,thd->khd", video_dscore, text_query3) * factor
    video_value_from_text = split_product("htk,thd->khd", video_prob, text_grad3)
    query_sum, key_sum, value_sum = lax.psum((query_part, text_key_acc, text_value_acc), "seq")
    text_query_grad = (
        query_sum
        + jnp.einsum("htk,khd->thd", text_dscore, text_key32, precision=HIGHEST_PRECISION) * factor
    )
    text_key_grad = (
        key_sum
        + jnp.einsum("htk,thd->khd", text_dscore, text_query32, precision=HIGHEST_PRECISION)
        * factor
    )
    text_value_grad = value_sum + jnp.einsum(
        "htk,thd->khd", text_prob, text_grad32, precision=HIGHEST_PRECISION
    )
    attended_rows = attended_blocks.reshape(token_rows, feature_width)
    query_grad_rows = query_grad_blocks.reshape(token_rows, feature_width)
    key_grad_rows = (
        own_key_grad.reshape(token_rows, feature_width)
        + video_key_from_text.reshape(token_rows, feature_width)
    ).astype(jnp.bfloat16)
    value_grad_rows = (
        own_value_grad.reshape(token_rows, feature_width)
        + video_value_from_text.reshape(token_rows, feature_width)
    ).astype(jnp.bfloat16)
    attended_video, video_query_grad, video_key_grad, video_value_grad = (
        lax.all_to_all(attended_rows, "head", split_axis=0, concat_axis=1, tiled=True),
        lax.all_to_all(query_grad_rows, "head", split_axis=0, concat_axis=1, tiled=True),
        lax.all_to_all(key_grad_rows, "head", split_axis=0, concat_axis=1, tiled=True),
        lax.all_to_all(value_grad_rows, "head", split_axis=0, concat_axis=1, tiled=True),
    )
    return (
        attended_video,
        video_query_grad,
        video_key_grad,
        video_value_grad,
        text_out.reshape(TXT, feature_width).astype(jnp.bfloat16),
        text_query_grad.reshape(TXT, feature_width).astype(jnp.bfloat16),
        text_key_grad.reshape(TXT, feature_width).astype(jnp.bfloat16),
        text_value_grad.reshape(TXT, feature_width).astype(jnp.bfloat16),
    )


def solution(mesh):
    placed = (
        P(("seq", "head"), None),
        P(("seq", "head"), None),
        P(("seq", "head"), None),
        P(("seq", "head"), None),
        P(None, "head"),
        P(None, "head"),
        P(None, "head"),
        P(None, "head"),
        P(),
        P(),
        P(),
    )
    return jax.shard_map(
        body,
        mesh=mesh,
        in_specs=placed,
        out_specs=(
            P(("seq", "head"), None),
            P(("seq", "head"), None),
            P(("seq", "head"), None),
            P(("seq", "head"), None),
            P(None, "head"),
            P(None, "head"),
            P(None, "head"),
            P(None, "head"),
        ),
        check_vma=False,
    )
```

profile of v0, /device:TPU:0, one launch (start us, length us, event | category | flops | bytes accessed | tf_op | source)
XLA Modules:
  0.0 900.4 jit_solution(9937720170638479781)
XLA Ops:
  50.8 66.3 %all-to-all-done.1 = bf16[8,256,768]{2,1,0:T(8,128)(2,1)} async-done(((bf16[8,256,768]{2,1,0:T(8,128)(2,1)}), bf16[8,256,768]{2,1,0:T(8,128)(2,1)}, u32[]{:S(2)}, u32[]{:S(2)}) %all-to-all-start.1) | async-done | bytes 3145760 | tf_op jit(solution)/shard_map/all_to_all | solution.py:183
  124.7 67.4 %all-to-all-done.3 = bf16[8,256,768]{2,1,0:T(8,128)(2,1)S(1)} async-done(((bf16[8,256,768]{2,1,0:T(8,128)(2,1)}), bf16[8,256,768]{2,1,0:T(8,128)(2,1)S(1)}, u32[]{:S(2)}, u32[]{:S(2)}) %all-to-all-start.3) | async-done | bytes 3145760 | tf_op jit(solution)/shard_map/all_to_all | solution.py:182
  212.1 13.7 %reshape.401 = bf16[4,1024,6,128]{3,2,1,0:T(8,128)(2,1)} reshape(bf16[32,128,768]{2,1,0:T(8,128)(2,1)} %gather_fusion.1) | data formatting | bytes 12582912 | tf_op jit(solution)/shard_map/while/body/eval_jaxpr/reshape | solution.py:175
  243.1 13.7 %reshape.400 = bf16[4,1024,6,128]{3,2,1,0:T(8,128)(2,1)} reshape(bf16[32,128,768]{2,1,0:T(8,128)(2,1)} %gather_fusion) | data formatting | bytes 12582912 | tf_op jit(solution)/shard_map/while/body/eval_jaxpr/reshape | solution.py:175
  256.8 11.5 %copy.380 = bf16[4,1024,6,128]{1,3,2,0:T(8,128)(2,1)} copy(bf16[4,1024,6,128]{3,2,1,0:T(8,128)(2,1)} %reshape.400) | data formatting | bytes 12582912 | tf_op jit(solution)/shard_map/while/body/eval_jaxpr/reshape | solution.py:175
  285.6 10.6 %bitcast_convert_fusion = (bf16[4,128,6,128]{1,3,2,0:T(8,128)(2,1)}, f32[4,6,128,128]{3,2,1,0:T(8,128)S(1)}) fusion(f32[4,6,1280,128]{3,2,1,0:T(8,128)} %copy-done.2, f32[4,6,128]{2,1,0:T(8,128)S(1)} %log_add_fusion, pred[4,1280]{1,0:T(4,128)(4,1)S(1)} %pad_add_fusion, bf16[4,256,6,128]{1,3,2,0:T(8,128)(2,1)S(1)} %broadcast_in_dim.182, ...), kind=kOutput, calls=%fused_computation.44 | convolution fusion | flops 1038483456 | bytes 25969664 | tf_op jit(solution)/shard_map/while/body/eval_jaxpr/bhtk,bkhd->bthd/dot_general | solution.py:36
  300.9 13.0 %fusion = bf16[4,6,128,1280]{2,3,1,0:T(8,128)(2,1)} fusion(f32[4,6,1280,128]{3,2,1,0:T(8,128)} %copy-done.2, bf16[4,128,6,128]{1,3,2,0:T(8,128)(2,1)S(1)} %bitcast.180, f32[4,6,128]{2,1,0:T(8,128)S(1)} %bitcast.208, f32[4,6,128]{2,1,0:T(8,128)S(1)} %log_add_fusion, pred[4,1280]{1,0:T(4,128)(4,1)S(1)} %pad_add_fusion, ...), kind=kOutput, calls=%fused_computation.9 | convolution fusion | flops 1045954560 | bytes 32273408 | tf_op jit(solution)/shard_map/while/body/eval_jaxpr/bthd,bkhd->bhtk/dot_general | solution.py:44
  326.8 11.1 %convolution_bitcast_fusion = f32[4,1280,6,128]{3,1,2,0:T(8,128)} fusion(bf16[4,128,6,128]{1,3,2,0:T(8,128)(2,1)S(1)} %bitcast.181, f32[4,6,1280,128]{3,2,1,0:T(8,128)} %copy-done.2, f32[4,6,128]{2,1,0:T(8,128)S(1)} %log_add_fusion, pred[4,1280]{1,0:T(4,128)(4,1)S(1)} %pad_add_fusion), kind=kOutput, calls=%fused_computation.19 | convolution fusion | flops 1022361600 | bytes 32261120 | tf_op jit(solution)/shard_map/while/body/eval_jaxpr/bhtk,bthd->bkhd/dot_general | solution.py:56
  337.9 10.4 %slice.43 = f32[4,1024,6,128]{3,1,2,0:T(8,128)} slice(f32[4,1280,6,128]{3,1,2,0:T(8,128)} %convolution_bitcast_fusion), slice={[0:4], [0:1024], [0:6], [0:128]} | slice | bytes 25165824 | tf_op jit(solution)/shard_map/while/body/eval_jaxpr/slice | solution.py:64
  348.3 17.8 %copy.498 = f32[4,1024,6,128]{3,2,1,0:T(8,128)} copy(f32[4,1024,6,128]{3,1,2,0:T(8,128)} %slice.43) | data formatting | bytes 25165824 | tf_op jit(solution)/shard_map/while/body/eval_jaxpr/reshape | solution.py:64
  366.1 16.1 %reshape.404 = f32[32,128,768]{2,1,0:T(8,128)} reshape(f32[4,1024,6,128]{3,2,1,0:T(8,128)} %copy.498) | data formatting | bytes 25165824 | tf_op jit(solution)/shard_map/while/body/eval_jaxpr/reshape | solution.py:64
  386.1 30.2 %scatter_fusion.2 = f32[20,128,768]{2,1,0:T(8,128)} fusion(f32[20,128,768]{2,1,0:T(8,128)} %broadcast.165.clone.1, s32[32]{0:T(128)S(1)} %reshape.345, f32[32,128,768]{2,1,0:T(8,128)} %reshape.404), kind=kCustom, calls=%fused_computation.4 | custom fusion | flops 3145728 | bytes 37748864 | tf_op jit(solution)/shard_map/while/body/eval_jaxpr/scatter-add | solution.py:66
  428.1 11.1 %multiply_bitcast_fusion = f32[4,1280,6,128]{3,1,2,0:T(8,128)} fusion(bf16[4,6,128,1280]{2,3,1,0:T(8,128)(2,1)} %fusion, bf16[4,128,6,128]{1,3,2,0:T(8,128)(2,1)} %bitcast.14), kind=kOutput, calls=%fused_computation.16 | convolution fusion | flops 1010565120 | bytes 24379392 | tf_op jit(solution)/shard_map/while/body/eval_jaxpr/bhtk,bthd->bkhd/dot_general | solution.py:53
  439.2 10.4 %slice.40 = f32[4,1024,6,128]{3,1,2,0:T(8,128)} slice(f32[4,1280,6,128]{3,1,2,0:T(8,128)} %multiply_bitcast_fusion), slice={[0:4], [0:1024], [0:6], [0:128]} | slice | bytes 25165824 | tf_op jit(solution)/shard_map/while/body/eval_jaxpr/slice | solution.py:64
  449.6 17.8 %copy.496 = f32[4,1024,6,128]{3,2,1,0:T(8,128)} copy(f32[4,1024,6,128]{3,1,2,0:T(8,128)} %slice.40) | data formatting | bytes 25165824 | tf_op jit(solution)/shard_map/while/body/eval_jaxpr/reshape | solution.py:64
  467.5 16.1 %reshape.402 = f32[32,128,768]{2,1,0:T(8,128)} reshape(f32[4,1024,6,128]{3,2,1,0:T(8,128)} %copy.496) | data formatting | bytes 25165824 | tf_op jit(solution)/shard_map/while/body/eval_jaxpr/reshape | solution.py:64
  487.5 30.1 %scatter_fusion = f32[20,128,768]{2,1,0:T(8,128)} fusion(f32[20,128,768]{2,1,0:T(8,128)} %broadcast.165.clone, s32[32]{0:T(128)S(1)} %reshape.345, f32[32,128,768]{2,1,0:T(8,128)} %reshape.402), kind=kCustom, calls=%fused_computation.2 | custom fusion | flops 3145728 | bytes 37748864 | tf_op jit(solution)/shard_map/while/body/eval_jaxpr/scatter-add | solution.py:66
  523.7 43.3 %all-to-all-done.10 = f32[8,256,768]{2,1,0:T(8,128)} async-done(((f32[8,256,768]{2,1,0:T(8,128)}), f32[8,256,768]{2,1,0:T(8,128)}, u32[]{:S(2)}, u32[]{:S(2)}) %all-to-all-start.10) | async-done | bytes 6291488 | tf_op jit(solution)/shard_map/all_to_all | solution.py:239
  583.2 103.5 %pmax.7 = f32[6,256]{1,0:T(8,128)} all-reduce(f32[6,256]{1,0:T(8,128)S(1)} %get-tuple-element.153), channel_id=1, replica_groups=mesh['seq'=8,'head'=4] {'seq'}, use_global_device_ids=true, to_apply=%region_12.13 | all-reduce | flops 1536 | bytes 12288 | tf_op jit(solution)/shard_map/pmax | solution.py:279
  692.2 44.9 %psum.35 = f32[6,256]{1,0:T(8,128)} all-reduce(f32[6,256]{1,0:T(8,128)S(1)} %fusion.9), channel_id=1, replica_groups=mesh['seq'=8,'head'=4] {'seq'}, use_global_device_ids=true, to_apply=%region_15.16 | all-reduce | flops 1536 | bytes 12288 | tf_op jit(solution)/shard_map/psum | solution.py:282
  747.5 32.2 %all-reduce.4.cloned.1.call-done = f32[256,6,128]{2,0,1:T(8,128)} async-done(((f32[256,6,128]{2,0,1:T(8,128)}), f32[256,6,128]{2,0,1:T(8,128)}) %all-reduce.4.cloned.1.call-update) | async-done | bytes 786448 | tf_op jit(solution)/shard_map/psum | solution.py:282
  812.2 9.2 %scatter_fusion.3 = f32[4,128,768]{2,1,0:T(8,128)S(1)} fusion(f32[4,128,768]{2,1,0:T(8,128)S(1)} %slice_add_fusion, s32[16]{0:T(128)S(1)} %copy-done.35, f32[16,128,768]{2,1,0:T(8,128)} %bitcast.47), kind=kCustom, calls=%fused_computation.5 | custom fusion | flops 1572864 | bytes 18874432 | tf_op jit(solution)/shard_map/scatter-add | solution.py:261
  833.5 29.9 %all-reduce.6.cloned.1.call-done = (f32[256,6,128]{2,0,1:T(8,128)}, f32[256,6,128]{2,0,1:T(8,128)}, f32[256,6,128]{0,2,1:T(8,128)}) async-done(((f32[256,6,128]{2,0,1:T(8,128)}, f32[256,6,128]{2,0,1:T(8,128)}, f32[256,6,128]{0,2,1:T(8,128)}), (f32[256,6,128]{2,0,1:T(8,128)}, f32[256,6,128]{2,0,1:T(8,128)}, f32[256,6,128]{0,2,1:T(8,128)})) %all-reduce.6.cloned.1.call-update) | async-done | bytes 2359312 | tf_op jit(solution)/shard_map/psum | solution.py:306
  868.4 9.2 %scatter_fusion.1 = f32[4,128,768]{2,1,0:T(8,128)S(1)} fusion(f32[4,128,768]{2,1,0:T(8,128)S(1)} %slice_add_fusion.1, s32[16]{0:T(128)S(1)} %copy-done.35, f32[16,128,768]{2,1,0:T(8,128)} %bitcast.41), kind=kCustom, calls=%fused_computation.3 | custom fusion | flops 1572864 | bytes 18874432 | tf_op jit(solution)/shard_map/scatter-add | solution.py:256
  (228 shorter events, 245.9 us)
Async XLA Ops:
  7.2 8.0 copy-start.33
  7.2 8.0 copy-start.38
  7.2 8.4 copy-start.26
  9.9 16.0 %all-to-all-start = ((bf16[128,4,768]{2,0,1:T(8,128)(2,1)}), bf16[128,4,768]{2,0,1:T(8,128)(2,1)S(1)}, u32[]{:S(2)}, u32[]{:S(2)}) async-start(bf16[128,4,768]{2,0,1:T(8,128)(2,1)} %copy.369), calls=%async_computation | async-start | bytes 1572864 | tf_op jit(solution)/shard_map/all_to_all | solution.py:90
  26.0 14.6 %all-to-all-start.2 = ((bf16[128,4,768]{2,0,1:T(8,128)(2,1)}), bf16[128,4,768]{2,0,1:T(8,128)(2,1)}, u32[]{:S(2)}, u32[]{:S(2)}) async-start(bf16[128,4,768]{2,0,1:T(8,128)(2,1)} %copy.382), calls=%async_computation.2 | async-start | bytes 1572864 | tf_op jit(solution)/shard_map/all_to_all | solution.py:89
  30.4 91.1 %copy-start.29 = (pred[8,8,2,4]{1,3,2,0:T(4,128)(4,1)}, pred[8,8,2,4]{1,3,2,0:T(4,128)(4,1)S(1)}, u32[]{:S(2)}) copy-start(pred[8,8,2,4]{1,3,2,0:T(4,128)(4,1)S(1)} %fusion.48) | copy-start | bytes 1540
  40.6 76.5 %all-to-all-start.1 = ((bf16[8,256,768]{2,1,0:T(8,128)(2,1)}), bf16[8,256,768]{2,1,0:T(8,128)(2,1)}, u32[]{:S(2)}, u32[]{:S(2)}) async-start(bf16[8,256,768]{2,1,0:T(8,128)(2,1)} %reshape.323), calls=%async_computation.1 | async-start | bytes 6291456 | tf_op jit(solution)/shard_map/all_to_all | solution.py:183
  50.8 70.0 %copy-start.39 = (s32[256]{0:T(256)S(1)}, s32[256]{0:T(256)}, u32[]{:S(2)}) copy-start(s32[256]{0:T(256)} %param.21) | copy-start | bytes 3076
  117.1 75.1 %all-to-all-start.3 = ((bf16[8,256,768]{2,1,0:T(8,128)(2,1)}), bf16[8,256,768]{2,1,0:T(8,128)(2,1)S(1)}, u32[]{:S(2)}, u32[]{:S(2)}) async-start(bf16[8,256,768]{2,1,0:T(8,128)(2,1)} %reshape.328), calls=%async_computation.3 | async-start | bytes 6291456 | tf_op jit(solution)/shard_map/all_to_all | solution.py:182
  192.2 76.1 %all-to-all-start.4 = ((bf16[128,4,768]{0,2,1:T(8,128)(2,1)}), bf16[128,4,768]{0,2,1:T(8,128)(2,1)}, u32[]{:S(2)}, u32[]{:S(2)}) async-start(bf16[128,4,768]{0,2,1:T(8,128)(2,1)} %bitcast.192), calls=%async_computation.4 | async-start | bytes 1572864 | tf_op jit(solution)/shard_map/all_to_all | solution.py:88
  197.8 8.5 copy-start.15
  225.7 7.5 copy-start.12
  256.8 15.7 %copy-start.25 = (bf16[256,6,128]{2,0,1:T(8,128)(2,1)S(1)}, bf16[256,6,128]{2,0,1:T(8,128)(2,1)}, u32[]{:S(2)}) copy-start(bf16[256,6,128]{2,0,1:T(8,128)(2,1)} %copy.385) | copy-start | bytes 1179652
  268.3 27.9 %all-to-all-start.6 = ((bf16[128,4,768]{0,2,1:T(8,128)(2,1)}), bf16[128,4,768]{0,2,1:T(8,128)(2,1)S(1)}, u32[]{:S(2)}, u32[]{:S(2)}) async-start(bf16[128,4,768]{0,2,1:T(8,128)(2,1)} %bitcast.20), calls=%async_computation.6 | async-start | bytes 1572864 | tf_op jit(solution)/shard_map/all_to_all | solution.py:91
  296.2 26.0 %all-to-all-start.5 = ((bf16[4,128,768]{1,2,0:T(8,128)(2,1)}), bf16[4,128,768]{1,2,0:T(8,128)(2,1)S(1)}, u32[]{:S(2)}, u32[]{:S(2)}) async-start(bf16[4,128,768]{1,2,0:T(8,128)(2,1)} %bitcast.203), calls=%async_computation.5 | async-start | bytes 1572864 | tf_op jit(solution)/shard_map/all_to_all | solution.py:330
  300.8 13.0 %copy-start.23 = (bf16[4,256,6,128]{3,1,2,0:T(8,128)(2,1)S(1)}, bf16[4,256,6,128]{3,1,2,0:T(8,128)(2,1)}, u32[]{:S(2)}) copy-start(bf16[4,256,6,128]{3,1,2,0:T(8,128)(2,1)} %copy-done.22) | copy-start | bytes 4718596
  322.2 15.7 %copy-start.20 = (bf16[4,128,768]{1,2,0:T(8,128)(2,1)}, bf16[4,128,768]{1,2,0:T(8,128)(2,1)S(1)}, u32[]{:S(2)}) copy-start(bf16[4,128,768]{1,2,0:T(8,128)(2,1)S(1)} %all-to-all-done.5) | copy-start | bytes 2359300
  322.2 100.2 %all-to-all-start.7 = ((bf16[4,128,768]{1,2,0:T(8,128)(2,1)}), bf16[4,128,768]{1,2,0:T(8,128)(2,1)S(1)}, u32[]{:S(2)}, u32[]{:S(2)}) async-start(bf16[4,128,768]{1,2,0:T(8,128)(2,1)} %bitcast.202), calls=%async_computation.7 | async-start | bytes 1572864 | tf_op jit(solution)/shard_map/all_to_all | solution.py:331
  423.4 143.7 %all-to-all-start.10 = ((f32[8,256,768]{2,1,0:T(8,128)}), f32[8,256,768]{2,1,0:T(8,128)}, u32[]{:S(2)}, u32[]{:S(2)}) async-start(f32[8,256,768]{2,1,0:T(8,128)} %bitcast.163), calls=%async_computation.10 | async-start | bytes 12582912 | tf_op jit(solution)/shard_map/all_to_all | solution.py:239
  567.1 255.4 %all-to-all-start.8 = ((f32[8,256,768]{2,1,0:T(8,128)}), f32[8,256,768]{2,1,0:T(8,128)}, u32[]{:S(2)}, u32[]{:S(2)}) async-start(f32[8,256,768]{2,1,0:T(8,128)} %bitcast.162), calls=%async_computation.8 | async-start | bytes 12582912 | tf_op jit(solution)/shard_map/all_to_all | solution.py:232
  572.0 207.6 %all-reduce.4.cloned.1.call-start = ((), (), s32[]{:S(2)}) async-start(), calls=%async_computation.12 | async-start | bytes 1572864 | tf_op jit(solution)/shard_map/psum | solution.py:282
  691.2 172.3 %all-reduce.6.cloned.1.call-start = ((), (), s32[]{:S(2)}) async-start(), calls=%async_computation.13 | async-start | bytes 4718592 | tf_op jit(solution)/shard_map/psum | solution.py:306
  822.4 56.1 %all-to-all-start.11 = ((bf16[4,128,768]{2,1,0:T(8,128)(2,1)}), bf16[4,128,768]{2,1,0:T(8,128)(2,1)}, u32[]{:S(2)}, u32[]{:S(2)}) async-start(bf16[4,128,768]{2,1,0:T(8,128)(2,1)} %convert_element_type.127), calls=%async_computation.11 | async-start | bytes 1572864 | tf_op jit(solution)/shard_map/all_to_all | solution.py:333
  878.5 13.3 %all-to-all-start.9 = ((bf16[4,128,768]{2,1,0:T(8,128)(2,1)}), bf16[4,128,768]{2,1,0:T(8,128)(2,1)S(1)}, u32[]{:S(2)}, u32[]{:S(2)}) async-start(bf16[4,128,768]{2,1,0:T(8,128)(2,1)} %convert_element_type.123), calls=%async_computation.9 | async-start | bytes 1572864 | tf_op jit(solution)/shard_map/all_to_all | solution.py:332
  (30 other events, 130.1 us)
Sparse Core Ops, SparseCore 0:
  691.3 88.3 all-reduce.3
  797.1 66.2 all-reduce.5
where the time goes:
time: 911 us; the launch traced here: 900 us
  waiting for transfers between devices  253 us (28%)
  local copies, waits for them, and re-layouts  228 us (25%)
  blocking collectives  148 us (16%)
  other arithmetic  109 us (12%)
  matrix products  94.3 us (10%)
  starting transfers between devices  53.4 us (6%)
  between operations  14.9 us (2%)
    pmax x1, blocking collectives, body(): lax.pmax(jnp.max(video_scores, axis=-1), 'seq')  104 us
    reshape x4, local copies, waits for them, and re-layouts, spread_grads(): grad_blk[:, :KT * TILE].reshape(block_tiles, KT, TILE, pool_total.shape[2])  67.9 us
    all_to_all x1, waiting for transfers between devices, body(): lax.all_to_all(send_keys, 'seq', split_axis=0, concat_axis=0, tiled=True)  67.4 us
    all_to_all x1, waiting for transfers between devices, body(): lax.all_to_all(send_values, 'seq', split_axis=0, concat_axis=0, tiled=True)  66.3 us
    scatter-add x2, other arithmetic, spread_grads(): pool_total.at[pool_slot].add(tile_part)  60.3 us
    reshape x4, local copies, waits for them, and re-layouts, block_rows(): picked = pool[slot_blk].reshape(block_tiles, KT * TILE, head_count, HD)  46.3 us
    psum x1, blocking collectives, body(): lax.psum((jnp.sum(video_exp, axis=-1), split_product('htk,khd->thd', vide...  44.9 us
    all_to_all x1, waiting for transfers between devices, body(): lax.all_to_all(value_acc[shard_tiles:].reshape(groups, MOST * TILE, featu...  43.3 us
  transfers between devices with their start and end apart: 14, of which 8 were waited for; matrix products, arithmetic and copies ran while one was open for 47% of the time, Pallas kernels for 0%

commit v1 on v0

--- a/solution.py
+++ b/solution.py
@@ -10,6 +10,22 @@
 MOST = 2
 NEGATIVE = -1e30
 HIGHEST_PRECISION = lax.Precision.HIGHEST
+
+
+def pairwise_exchange(value, axis, split, join):
+    ways, here = (lax.axis_size(axis), lax.axis_index(axis))
+    width = value.shape[split] // ways
+    shape = list(value.shape)
+    shape[split] = width
+    height = shape[join]
+    shape[join] = height * ways
+    full = jnp.zeros(shape, value.dtype)
+    for mask in range(ways):
+        part = lax.dynamic_slice_in_dim(value, (here ^ mask) * width, width, axis=split)
+        if mask:
+            part = lax.ppermute(part, axis, [(d, d ^ mask) for d in range(ways)])
+        full = lax.dynamic_update_slice_in_dim(full, part, (here ^ mask) * height, axis=join)
+    return full
 
 
 def split_product(form, weights, data):
@@ -180,7 +196,7 @@
     pool_keys, pool_values = build_pool(
         (
             lax.all_to_all(send_keys, "seq", split_axis=0, concat_axis=0, tiled=True),
-            lax.all_to_all(send_values, "seq", split_axis=0, concat_axis=0, tiled=True),
+            pairwise_exchange(send_values, "seq", 0, 0),
         )
     )
     start = (

time: 911 us -> 1010 us (1.11)
  local copies, waits for them, and re-layouts: 228 us -> 269 us
  waiting for transfers between devices: 253 us -> 279 us
  starting transfers between devices: 53.4 us -> 69.3 us
    ppermute x0 -> x7, waiting for transfers between devices: none -> 98.7 us  [pairwise_exchange(): part = lax.ppermute(part, axis, [(d, d ^ mask) for d in range(ways)])]
    all_to_all x1, waiting for transfers between devices: 67.4 us -> 0.01 us  [body(): lax.all_to_all(send_keys, 'seq', split_axis=0, concat_axis=0, tiled=True)]
    reshape x4 -> x6, local copies, waits for them, and re-layouts: 46.3 us -> 67.3 us  [block_rows(): picked = pool[slot_blk].reshape(block_tiles, KT * TILE, head_count, HD)]
    ppermute x0 -> x7, starting transfers between devices: none -> 11.7 us  [pairwise_exchange(): part = lax.ppermute(part, axis, [(d, d ^ mask) for d in range(ways)])]
    dynamic_update_slice x0 -> x7, local copies, waits for them, and re-layouts: none -> 10.4 us  [pairwise_exchange(): lax.dynamic_update_slice_in_dim(full, part, (here ^ mask) * height, axis=...]
    unnamed x98 -> x105, local copies, waits for them, and re-layouts: 23.1 us -> 17.2 us
  transfers between devices with their start and end apart: 14 -> 21, of which waited for: 8 -> 10; matrix products, arithmetic and copies ran while one was open for 47% -> 47% of each run, Pallas kernels for 0% -> 0%
where the time goes in v1:
time: 1010 us; the launch traced here: 994 us
  waiting for transfers between devices  279 us (28%)
  local copies, waits for them, and re-layouts  269 us (27%)
  blocking collectives  149 us (15%)
  other arithmetic  112 us (11%)
  matrix products  100 us (10%)
  starting transfers between devices  69.3 us (7%)
  between operations  15 us (1%)
    pmax x1, blocking collectives, body(): lax.pmax(jnp.max(video_scores, axis=-1), 'seq')  104 us
    ppermute x7, waiting for transfers between devices, pairwise_exchange(): part = lax.ppermute(part, axis, [(d, d ^ mask) for d in range(ways)])  98.7 us
    reshape x4, local copies, waits for them, and re-layouts, spread_grads(): grad_blk[:, :KT * TILE].reshape(block_tiles, KT, TILE, pool_total.shape[2])  67.9 us
    reshape x6, local copies, waits for them, and re-layouts, block_rows(): picked = pool[slot_blk].reshape(block_tiles, KT * TILE, head_count, HD)  67.3 us
    all_to_all x1, waiting for transfers between devices, body(): lax.all_to_all(send_values, 'seq', split_axis=0, concat_axis=0, tiled=True)  64.4 us
    scatter-add x2, other arithmetic, spread_grads(): pool_total.at[pool_slot].add(tile_part)  60.3 us
    psum x1, blocking collectives, body(): lax.psum((jnp.sum(video_exp, axis=-1), split_product('htk,khd->thd', vide...  44.8 us
    all_to_all x1, waiting for transfers between devices, body(): lax.all_to_all(value_acc[shard_tiles:].reshape(groups, MOST * TILE, featu...  43.7 us
  transfers between devices with their start and end apart: 21, of which 10 were waited for; matrix products, arithmetic and copies ran while one was open for 47% of the time, Pallas kernels for 0%

profile of v1, /device:TPU:0, one launch (start us, length us, event | category | flops | bytes accessed | tf_op | source)
XLA Modules:
  0.0 993.9 jit_solution(6511057517692888082)
XLA Ops:
  51.9 64.4 %all-to-all-done.5 = bf16[8,256,768]{2,1,0:T(8,128)(2,1)} async-done(((bf16[8,256,768]{2,1,0:T(8,128)(2,1)}), bf16[8,256,768]{2,1,0:T(8,128)(2,1)}, u32[]{:S(2)}, u32[]{:S(2)}) %all-to-all-start.5) | async-done | bytes 3145760 | tf_op jit(solution)/shard_map/all_to_all | solution.py:224
  142.5 47.1 %collective-permute-done.1 = bf16[1,256,768]{2,1,0:T(8,128)(2,1)} collective-permute-done((bf16[1,256,768]{2,1,0:T(8,128)(2,1)}, bf16[1,256,768]{2,1,0:T(8,128)(2,1)}, u32[]{:S(2)}, u32[]{:S(2)}) %collective-permute-start.1) | collective-permute-done | bytes 393248 | tf_op jit(solution)/shard_map/ppermute | solution.py:26
  197.2 37.7 %collective-permute-done.3 = bf16[1,256,768]{2,1,0:T(8,128)(2,1)} collective-permute-done((bf16[1,256,768]{2,1,0:T(8,128)(2,1)}, bf16[1,256,768]{2,1,0:T(8,128)(2,1)}, u32[]{:S(2)}, u32[]{:S(2)}) %collective-permute-start.3) | collective-permute-done | bytes 393248 | tf_op jit(solution)/shard_map/ppermute | solution.py:26
  236.7 13.8 %collective-permute-done.4 = bf16[1,256,768]{2,1,0:T(8,128)(2,1)S(1)} collective-permute-done((bf16[1,256,768]{2,1,0:T(8,128)(2,1)}, bf16[1,256,768]{2,1,0:T(8,128)(2,1)S(1)}, u32[]{:S(2)}, u32[]{:S(2)}) %collective-permute-start.4) | collective-permute-done | bytes 393248 | tf_op jit(solution)/shard_map/ppermute | solution.py:26
  267.4 13.7 %reshape.417 = bf16[4,1024,6,128]{3,2,1,0:T(8,128)(2,1)} reshape(bf16[32,128,768]{2,1,0:T(8,128)(2,1)} %gather_fusion.1) | data formatting | bytes 12582912 | tf_op jit(solution)/shard_map/while/body/eval_jaxpr/reshape | solution.py:191
  299.6 13.7 %reshape.416 = bf16[4,1024,6,128]{3,2,1,0:T(8,128)(2,1)} reshape(bf16[32,128,768]{2,1,0:T(8,128)(2,1)} %gather_fusion) | data formatting | bytes 12582912 | tf_op jit(solution)/shard_map/while/body/eval_jaxpr/reshape | solution.py:191
  313.3 11.5 %copy.389 = bf16[4,1024,6,128]{1,3,2,0:T(8,128)(2,1)} copy(bf16[4,1024,6,128]{3,2,1,0:T(8,128)(2,1)} %reshape.416) | data formatting | bytes 12582912 | tf_op jit(solution)/shard_map/while/body/eval_jaxpr/reshape | solution.py:191
  344.5 10.9 %bitcast_convert_fusion = (bf16[4,128,6,128]{1,3,2,0:T(8,128)(2,1)}, f32[4,6,128,128]{3,2,1,0:T(8,128)}) fusion(f32[4,6,1280,128]{3,2,1,0:T(8,128)} %copy-done.2, f32[4,6,128]{2,1,0:T(8,128)S(1)} %log_add_fusion, pred[4,1280]{1,0:T(4,128)(4,1)S(1)} %pad_add_fusion, bf16[4,256,6,128]{1,3,2,0:T(8,128)(2,1)S(1)} %broadcast_in_dim.186, ...), kind=kOutput, calls=%fused_computation.51 | convolution fusion | flops 1038483456 | bytes 25969664 | tf_op jit(solution)/shard_map/while/body/eval_jaxpr/bhtk,bkhd->bthd/dot_general | solution.py:52
  361.1 13.7 %reshape.418 = bf16[4,1024,6,128]{3,2,1,0:T(8,128)(2,1)} reshape(bf16[32,128,768]{2,1,0:T(8,128)(2,1)} %gather_fusion.2) | data formatting | bytes 12582912 | tf_op jit(solution)/shard_map/while/body/eval_jaxpr/reshape | solution.py:191
  389.5 12.2 %fusion = bf16[4,6,128,1280]{2,3,1,0:T(8,128)(2,1)} fusion(f32[4,6,1280,128]{3,2,1,0:T(8,128)} %copy-done.2, bf16[4,128,6,128]{1,3,2,0:T(8,128)(2,1)S(1)} %bitcast.185, bf16[4,256,6,128]{3,1,2,0:T(8,128)(2,1)} %broadcast_in_dim.186.clone, bf16[4,1024,6,128]{3,1,2,0:T(8,128)(2,1)} %copy.401, f32[4,6,128]{2,1,0:T(8,128)S(1)} %bitcast.215, ...), kind=kOutput, calls=%fused_computation.10 | convolution fusion | flops 1045954560 | bytes 32273408 | tf_op jit(solution)/shard_map/while/body/eval_jaxpr/bthd,bkhd->bhtk/dot_general | solution.py:60
  415.2 11.1 %convolution_bitcast_fusion = f32[4,1280,6,128]{3,1,2,0:T(8,128)} fusion(bf16[4,128,6,128]{1,3,2,0:T(8,128)(2,1)S(1)} %bitcast.186, f32[4,6,1280,128]{3,2,1,0:T(8,128)} %copy-done.2, f32[4,6,128]{2,1,0:T(8,128)S(1)} %copy-done.33, pred[4,1280]{1,0:T(4,128)(4,1)S(1)} %pad_add_fusion), kind=kOutput, calls=%fused_computation.20 | convolution fusion | flops 1022361600 | bytes 32261120 | tf_op jit(solution)/shard_map/while/body/eval_jaxpr/bhtk,bthd->bkhd/dot_general | solution.py:72
  436.6 17.8 %copy.510 = f32[4,1024,6,128]{3,2,1,0:T(8,128)} copy(f32[4,1024,6,128]{3,1,2,0:T(8,128)} %slice.45) | data formatting | bytes 25165824 | tf_op jit(solution)/shard_map/while/body/eval_jaxpr/reshape | solution.py:80
  454.4 16.0 %reshape.421 = f32[32,128,768]{2,1,0:T(8,128)} reshape(f32[4,1024,6,128]{3,2,1,0:T(8,128)} %copy.510) | data formatting | bytes 25165824 | tf_op jit(solution)/shard_map/while/body/eval_jaxpr/reshape | solution.py:80
  474.4 30.3 %scatter_fusion.2 = f32[20,128,768]{2,1,0:T(8,128)} fusion(f32[20,128,768]{2,1,0:T(8,128)} %broadcast.165.clone.1, s32[32]{0:T(128)S(1)} %reshape.351, f32[32,128,768]{2,1,0:T(8,128)} %reshape.421), kind=kCustom, calls=%fused_computation.5 | custom fusion | flops 3145728 | bytes 37748864 | tf_op jit(solution)/shard_map/while/body/eval_jaxpr/scatter-add | solution.py:82
  521.5 11.0 %multiply_bitcast_fusion = f32[4,1280,6,128]{3,1,2,0:T(8,128)} fusion(bf16[4,6,128,1280]{2,3,1,0:T(8,128)(2,1)} %fusion, bf16[4,128,6,128]{1,3,2,0:T(8,128)(2,1)S(1)} %bitcast.195), kind=kOutput, calls=%fused_computation.17 | convolution fusion | flops 1010565120 | bytes 24379392 | tf_op jit(solution)/shard_map/while/body/eval_jaxpr/bhtk,bthd->bkhd/dot_general | solution.py:69
  532.5 10.4 %slice.42 = f32[4,1024,6,128]{3,1,2,0:T(8,128)} slice(f32[4,1280,6,128]{3,1,2,0:T(8,128)} %multiply_bitcast_fusion), slice={[0:4], [0:1024], [0:6], [0:128]} | slice | bytes 25165824 | tf_op jit(solution)/shard_map/while/body/eval_jaxpr/slice | solution.py:80
  542.8 17.8 %copy.508 = f32[4,1024,6,128]{3,2,1,0:T(8,128)} copy(f32[4,1024,6,128]{3,1,2,0:T(8,128)} %slice.42) | data formatting | bytes 25165824 | tf_op jit(solution)/shard_map/while/body/eval_jaxpr/reshape | solution.py:80
  560.7 16.1 %reshape.419 = f32[32,128,768]{2,1,0:T(8,128)} reshape(f32[4,1024,6,128]{3,2,1,0:T(8,128)} %copy.508) | data formatting | bytes 25165824 | tf_op jit(solution)/shard_map/while/body/eval_jaxpr/reshape | solution.py:80
  580.7 30.0 %scatter_fusion = f32[20,128,768]{2,1,0:T(8,128)} fusion(f32[20,128,768]{2,1,0:T(8,128)} %broadcast.165.clone, s32[32]{0:T(128)S(1)} %reshape.351, f32[32,128,768]{2,1,0:T(8,128)} %reshape.419), kind=kCustom, calls=%fused_computation.3 | custom fusion | flops 3145728 | bytes 37748864 | tf_op jit(solution)/shard_map/while/body/eval_jaxpr/scatter-add | solution.py:82
  616.8 43.7 %all-to-all-done.10 = f32[8,256,768]{2,1,0:T(8,128)} async-done(((f32[8,256,768]{2,1,0:T(8,128)}), f32[8,256,768]{2,1,0:T(8,128)}, u32[]{:S(2)}, u32[]{:S(2)}) %all-to-all-start.10) | async-done | bytes 6291488 | tf_op jit(solution)/shard_map/all_to_all | solution.py:255
  675.8 104.4 %pmax.7 = f32[6,256]{1,0:T(8,128)} all-reduce(f32[6,256]{1,0:T(8,128)S(1)} %get-tuple-element.163), channel_id=1, replica_groups=mesh['seq'=8,'head'=4] {'seq'}, use_global_device_ids=true, to_apply=%region_12.13 | all-reduce | flops 1536 | bytes 12288 | tf_op jit(solution)/shard_map/pmax | solution.py:295
  785.6 44.8 %psum.35 = f32[6,256]{1,0:T(8,128)} all-reduce(f32[6,256]{1,0:T(8,128)S(1)} %fusion.15), channel_id=1, replica_groups=mesh['seq'=8,'head'=4] {'seq'}, use_global_device_ids=true, to_apply=%region_15.16 | all-reduce | flops 1536 | bytes 12288 | tf_op jit(solution)/shard_map/psum | solution.py:298
  840.9 32.2 %all-reduce.4.cloned.1.call-done = f32[256,6,128]{2,0,1:T(8,128)} async-done(((f32[256,6,128]{2,0,1:T(8,128)}), f32[256,6,128]{2,0,1:T(8,128)}) %all-reduce.4.cloned.1.call-update) | async-done | bytes 786448 | tf_op jit(solution)/shard_map/psum | solution.py:298
  927.0 29.9 %all-reduce.6.cloned.1.call-done = (f32[256,6,128]{2,0,1:T(8,128)}, f32[256,6,128]{2,0,1:T(8,128)}, f32[256,6,128]{0,2,1:T(8,128)}) async-done(((f32[256,6,128]{2,0,1:T(8,128)}, f32[256,6,128]{2,0,1:T(8,128)}, f32[256,6,128]{0,2,1:T(8,128)}), (f32[256,6,128]{2,0,1:T(8,128)}, f32[256,6,128]{2,0,1:T(8,128)}, f32[256,6,128]{0,2,1:T(8,128)})) %all-reduce.6.cloned.1.call-update) | async-done | bytes 2359312 | tf_op jit(solution)/shard_map/psum | solution.py:322
  (262 shorter events, 324.6 us)
Async XLA Ops:
  9.9 16.0 %all-to-all-start = ((bf16[128,4,768]{2,0,1:T(8,128)(2,1)}), bf16[128,4,768]{2,0,1:T(8,128)(2,1)S(1)}, u32[]{:S(2)}, u32[]{:S(2)}) async-start(bf16[128,4,768]{2,0,1:T(8,128)(2,1)} %copy.378), calls=%async_computation | async-start | bytes 1572864 | tf_op jit(solution)/shard_map/all_to_all | solution.py:106
  26.0 262.6 %copy-start.8 = (bf16[128,4,768]{2,0,1:T(8,128)(2,1)}, bf16[128,4,768]{2,0,1:T(8,128)(2,1)S(1)}, u32[]{:S(2)}) copy-start(bf16[128,4,768]{2,0,1:T(8,128)(2,1)S(1)} %all-to-all-done) | copy-start | bytes 2359300
  26.0 13.8 %all-to-all-start.1 = ((bf16[128,4,768]{2,0,1:T(8,128)(2,1)}), bf16[128,4,768]{2,0,1:T(8,128)(2,1)S(1)}, u32[]{:S(2)}, u32[]{:S(2)}) async-start(bf16[128,4,768]{2,0,1:T(8,128)(2,1)} %copy.391), calls=%async_computation.1 | async-start | bytes 1572864 | tf_op jit(solution)/shard_map/all_to_all | solution.py:105
  39.8 217.8 %copy-start.13 = (bf16[128,4,768]{2,0,1:T(8,128)(2,1)}, bf16[128,4,768]{2,0,1:T(8,128)(2,1)S(1)}, u32[]{:S(2)}) copy-start(bf16[128,4,768]{2,0,1:T(8,128)(2,1)S(1)} %all-to-all-done.1) | copy-start | bytes 2359300
  39.8 76.5 %all-to-all-start.5 = ((bf16[8,256,768]{2,1,0:T(8,128)(2,1)}), bf16[8,256,768]{2,1,0:T(8,128)(2,1)}, u32[]{:S(2)}, u32[]{:S(2)}) async-start(bf16[8,256,768]{2,1,0:T(8,128)(2,1)} %reshape.327), calls=%async_computation.5 | async-start | bytes 6291456 | tf_op jit(solution)/shard_map/all_to_all | solution.py:224
  116.3 135.8 %all-to-all-start.2 = ((bf16[8,256,768]{2,1,0:T(8,128)(2,1)}), bf16[8,256,768]{2,1,0:T(8,128)(2,1)}, u32[]{:S(2)}, u32[]{:S(2)}) async-start(bf16[8,256,768]{2,1,0:T(8,128)(2,1)} %reshape.332), calls=%async_computation.2 | async-start | bytes 6291456 | tf_op jit(solution)/shard_map/all_to_all | solution.py:198
  127.8 10.9 %collective-permute-start = (bf16[1,256,768]{2,1,0:T(8,128)(2,1)}, bf16[1,256,768]{2,1,0:T(8,128)(2,1)}, u32[]{:S(2)}, u32[]{:S(2)}) collective-permute-start(bf16[1,256,768]{2,1,0:T(8,128)(2,1)} %get-tuple-element.151), channel_id=1, source_target_pairs={{0,4},{4,0},{8,12},{12,8},{16,20},{20,16},{24,28},{28,24},{1,5},{5... | collective-permute-start | bytes 1179656 | tf_op jit(solution)/shard_map/ppermute | solution.py:26
  128.3 67.1 %collective-permute-start.2 = (bf16[1,256,768]{2,1,0:T(8,128)(2,1)}, bf16[1,256,768]{2,1,0:T(8,128)(2,1)}, u32[]{:S(2)}, u32[]{:S(2)}) collective-permute-start(bf16[1,256,768]{2,1,0:T(8,128)(2,1)} %get-tuple-element.149), channel_id=1, source_target_pairs={{0,12},{4,8},{8,4},{12,0},{16,28},{20,24},{24,20},{28,16},{1,13},{... | collective-permute-start | bytes 1179656 | tf_op jit(solution)/shard_map/ppermute | solution.py:26
  130.0 59.5 %collective-permute-start.1 = (bf16[1,256,768]{2,1,0:T(8,128)(2,1)}, bf16[1,256,768]{2,1,0:T(8,128)(2,1)}, u32[]{:S(2)}, u32[]{:S(2)}) collective-permute-start(bf16[1,256,768]{2,1,0:T(8,128)(2,1)} %get-tuple-element.150), channel_id=1, source_target_pairs={{0,8},{4,12},{8,0},{12,4},{16,24},{20,28},{24,16},{28,20},{1,9},{5... | collective-permute-start | bytes 1179656 | tf_op jit(solution)/shard_map/ppermute | solution.py:26
  130.3 104.7 %collective-permute-start.3 = (bf16[1,256,768]{2,1,0:T(8,128)(2,1)}, bf16[1,256,768]{2,1,0:T(8,128)(2,1)}, u32[]{:S(2)}, u32[]{:S(2)}) collective-permute-start(bf16[1,256,768]{2,1,0:T(8,128)(2,1)} %get-tuple-element.148), channel_id=1, source_target_pairs={{0,16},{4,20},{8,24},{12,28},{16,0},{20,4},{24,8},{28,12},{1,17},{... | collective-permute-start | bytes 1179656 | tf_op jit(solution)/shard_map/ppermute | solution.py:26
  134.3 210.0 %copy-start.19 = (bf16[256,768]{0,1:T(8,128)(2,1)}, bf16[256,768]{0,1:T(8,128)(2,1)S(1)}, u32[]{:S(2)}) copy-start(bf16[256,768]{0,1:T(8,128)(2,1)S(1)} %copy.388) | copy-start | bytes 1179652
  138.0 117.8 %collective-permute-start.6 = (bf16[1,256,768]{2,1,0:T(8,128)(2,1)}, bf16[1,256,768]{2,1,0:T(8,128)(2,1)}, u32[]{:S(2)}, u32[]{:S(2)}) collective-permute-start(bf16[1,256,768]{2,1,0:T(8,128)(2,1)} %get-tuple-element.145), channel_id=1, source_target_pairs={{0,28},{4,24},{8,20},{12,16},{16,12},{20,8},{24,4},{28,0},{1,29},{... | collective-permute-start | bytes 1179656 | tf_op jit(solution)/shard_map/ppermute | solution.py:26
  138.6 111.9 %collective-permute-start.4 = (bf16[1,256,768]{2,1,0:T(8,128)(2,1)}, bf16[1,256,768]{2,1,0:T(8,128)(2,1)S(1)}, u32[]{:S(2)}, u32[]{:S(2)}) collective-permute-start(bf16[1,256,768]{2,1,0:T(8,128)(2,1)} %get-tuple-element.147), channel_id=1, source_target_pairs={{0,20},{4,16},{8,28},{12,24},{16,4},{20,0},{24,12},{28,8},{1,21},{... | collective-permute-start | bytes 1179656 | tf_op jit(solution)/shard_map/ppermute | solution.py:26
  189.6 61.8 %collective-permute-start.5 = (bf16[1,256,768]{2,1,0:T(8,128)(2,1)}, bf16[1,256,768]{2,1,0:T(8,128)(2,1)S(1)}, u32[]{:S(2)}, u32[]{:S(2)}) collective-permute-start(bf16[1,256,768]{2,1,0:T(8,128)(2,1)} %get-tuple-element.146), channel_id=1, source_target_pairs={{0,24},{4,28},{8,16},{12,20},{16,8},{20,12},{24,0},{28,4},{1,25},{... | collective-permute-start | bytes 1179656 | tf_op jit(solution)/shard_map/ppermute | solution.py:26
  252.1 72.7 %all-to-all-start.3 = ((bf16[128,4,768]{0,2,1:T(8,128)(2,1)}), bf16[128,4,768]{0,2,1:T(8,128)(2,1)S(1)}, u32[]{:S(2)}, u32[]{:S(2)}) async-start(bf16[128,4,768]{0,2,1:T(8,128)(2,1)} %bitcast.200), calls=%async_computation.3 | async-start | bytes 1572864 | tf_op jit(solution)/shard_map/all_to_all | solution.py:104
  324.8 57.4 %all-to-all-start.6 = ((bf16[128,4,768]{0,2,1:T(8,128)(2,1)}), bf16[128,4,768]{0,2,1:T(8,128)(2,1)S(1)}, u32[]{:S(2)}, u32[]{:S(2)}) async-start(bf16[128,4,768]{0,2,1:T(8,128)(2,1)} %bitcast.21), calls=%async_computation.6 | async-start | bytes 1572864 | tf_op jit(solution)/shard_map/all_to_all | solution.py:107
  382.2 28.4 %all-to-all-start.4 = ((bf16[4,128,768]{1,2,0:T(8,128)(2,1)}), bf16[4,128,768]{1,2,0:T(8,128)(2,1)S(1)}, u32[]{:S(2)}, u32[]{:S(2)}) async-start(bf16[4,128,768]{1,2,0:T(8,128)(2,1)} %bitcast.17), calls=%async_computation.4 | async-start | bytes 1572864 | tf_op jit(solution)/shard_map/all_to_all | solution.py:346
  410.6 100.3 %all-to-all-start.7 = ((bf16[4,128,768]{1,2,0:T(8,128)(2,1)}), bf16[4,128,768]{1,2,0:T(8,128)(2,1)S(1)}, u32[]{:S(2)}, u32[]{:S(2)}) async-start(bf16[4,128,768]{1,2,0:T(8,128)(2,1)} %bitcast.210), calls=%async_computation.7 | async-start | bytes 1572864 | tf_op jit(solution)/shard_map/all_to_all | solution.py:347
  511.8 148.7 %all-to-all-start.10 = ((f32[8,256,768]{2,1,0:T(8,128)}), f32[8,256,768]{2,1,0:T(8,128)}, u32[]{:S(2)}, u32[]{:S(2)}) async-start(f32[8,256,768]{2,1,0:T(8,128)} %bitcast.166), calls=%async_computation.10 | async-start | bytes 12582912 | tf_op jit(solution)/shard_map/all_to_all | solution.py:255
  660.5 255.5 %all-to-all-start.8 = ((f32[8,256,768]{2,1,0:T(8,128)}), f32[8,256,768]{2,1,0:T(8,128)}, u32[]{:S(2)}, u32[]{:S(2)}) async-start(f32[8,256,768]{2,1,0:T(8,128)} %bitcast.165), calls=%async_computation.8 | async-start | bytes 12582912 | tf_op jit(solution)/shard_map/all_to_all | solution.py:248
  665.5 207.6 %all-reduce.4.cloned.1.call-start = ((), (), s32[]{:S(2)}) async-start(), calls=%async_computation.12 | async-start | bytes 1572864 | tf_op jit(solution)/shard_map/psum | solution.py:298
  784.7 172.3 %all-reduce.6.cloned.1.call-start = ((), (), s32[]{:S(2)}) async-start(), calls=%async_computation.13 | async-start | bytes 4718592 | tf_op jit(solution)/shard_map/psum | solution.py:322
  916.0 56.1 %all-to-all-start.11 = ((bf16[4,128,768]{2,1,0:T(8,128)(2,1)}), bf16[4,128,768]{2,1,0:T(8,128)(2,1)}, u32[]{:S(2)}, u32[]{:S(2)}) async-start(bf16[4,128,768]{2,1,0:T(8,128)(2,1)} %convert_element_type.127), calls=%async_computation.11 | async-start | bytes 1572864 | tf_op jit(solution)/shard_map/all_to_all | solution.py:349
  972.0 13.3 %all-to-all-start.9 = ((bf16[4,128,768]{2,1,0:T(8,128)(2,1)}), bf16[4,128,768]{2,1,0:T(8,128)(2,1)S(1)}, u32[]{:S(2)}, u32[]{:S(2)}) async-start(bf16[4,128,768]{2,1,0:T(8,128)(2,1)} %convert_element_type.123), calls=%async_computation.9 | async-start | bytes 1572864 | tf_op jit(solution)/shard_map/all_to_all | solution.py:348
  (40 other events, 424.9 us)
Sparse Core Ops, SparseCore 0:
  784.8 88.3 all-reduce.3
  890.7 66.2 all-reduce.5
